TPU v7x, 32 devices: a whole 2x2x4 slice. The times are simulated.
32 devices in a mesh: groups: 2 (over y), seq: 16 (over z, x, core).
Axes of the slice: x: 2, y: 2, z: 4, core: 2. Of those that a mesh axis runs over, the one named last changes fastest.
Arguments:
- video_q: bfloat16 [8192, 1536], P(('groups', 'seq')), parts along dimension 0, may hold values from -9 to 9
- video_k: bfloat16 [8192, 1536], P(('groups', 'seq')), parts along dimension 0, may hold values from -9 to 9
- video_v: bfloat16 [8192, 1536], P(('groups', 'seq')), parts along dimension 0, may hold values from -6 to 6
- audio_query_rows: bfloat16 [2048, 1536], P(('groups', 'seq')), parts along dimension 0, may hold values from -9 to 9
- audio_k: bfloat16 [2048, 1536], P(('groups', 'seq')), parts along dimension 0, may hold values from -9 to 9
- audio_v: bfloat16 [2048, 1536], P(('groups', 'seq')), parts along dimension 0, may hold values from -6 to 6
- video_start: int32 [32], P(('groups', 'seq')), parts along dimension 0, may hold values from 0 to 15, as said below
- video_count: int32 [32], P(('groups', 'seq')), parts along dimension 0, may hold values from 1 to 5, as said below
- audio_start: int32 [32], P(('groups', 'seq')), parts along dimension 0, may hold values from 0 to 15, as said below
- audio_count: int32 [32], P(('groups', 'seq')), parts along dimension 0, may hold values from 1 to 5, as said below
Outputs:
- video_out: bfloat16 [8192, 1536], P(('groups', 'seq')), parts along dimension 0
- audio_out: bfloat16 [2048, 1536], P(('groups', 'seq')), parts along dimension 0
There are 2 independent parts, one for each index of `groups`. A program takes and returns all parts, laid end to end along the dimension named above; each array names one. Nothing has to cross between parts.
Inputs may be any that keep to these rules, and one draw needn't show every extreme that they name: `video_start`: video block i's band of audio blocks contains block i and lies within blocks i - 2 to i + 2. `video_count`: the band counts blocks within the clip; some video block's band holds 5 blocks. `audio_start`: audio block j's band of video blocks contains block j and lies within blocks j - 2 to j + 2. `audio_count`: the band counts blocks within the clip; some audio block's band holds 5 blocks.
All inputs are finite; a program needn't handle non-finite values.
Results may differ from a plain program's by a relative error of at most 0.0045.
Values may be sent and summed in bfloat16 or wider, within the bound.
No kernel may reach another device: no remote copies, remote signals or barrier semaphores. Data moves between devices by JAX's collectives and lax.ppermute only.
A program may use at most 64 MiB of HBM per device.

v0:
```python
import math

import jax
import jax.numpy as jnp
from jax import lax
from jax.sharding import PartitionSpec as P

HEADS = 12
HEAD_DIM = 128
RADIUS = 2


def shifted(shard, axis, by):
    peers = lax.axis_size(axis)
    pairs = [(i, i + by) for i in range(peers) if 0 <= i + by < peers]
    return lax.ppermute(shard, axis, pairs)


def partial_results(queries, keys, values):
    row_count = queries.shape[0]
    key_count = keys.shape[0]
    query_heads = queries.reshape(row_count, HEADS, HEAD_DIM)
    key_heads = keys.reshape(key_count, HEADS, HEAD_DIM)
    value_heads = values.reshape(key_count, HEADS, HEAD_DIM)
    scores = jnp.einsum(
        "qhd,khd->hqk", query_heads, key_heads, preferred_element_type=jnp.float32
    ) * (1.0 / math.sqrt(HEAD_DIM))
    maxima = jnp.max(scores, axis=-1)
    raised = jnp.exp(scores - maxima[..., None])
    totals = jnp.sum(raised, axis=-1)
    weights_bf = raised.astype(jnp.bfloat16)
    numerators = jnp.einsum(
        "hqk,khd->qhd", weights_bf, value_heads, preferred_element_type=jnp.float32
    )
    return (numerators.reshape(row_count, HEADS * HEAD_DIM), maxima, totals)


def merge_in(state, arriving, in_range):
    numerators, maxima, totals = state
    part_numerators, part_maxima, part_totals = arriving
    row_count = numerators.shape[0]
    highest = jnp.where(in_range, jnp.maximum(maxima, part_maxima), maxima)
    rescale = jnp.exp(maxima - highest)
    received_blocks = jnp.where(in_range, jnp.exp(part_maxima - highest), 0.0)
    totals = totals * rescale + part_totals * received_blocks
    merged = numerators.reshape(row_count, HEADS, HEAD_DIM) * rescale.T[:, :, None]
    merged = (
        merged + part_numerators.reshape(row_count, HEADS, HEAD_DIM) * received_blocks.T[:, :, None]
    )
    return (merged.reshape(row_count, HEADS * HEAD_DIM), highest, totals)


def finish(state):
    numerators, maxima, totals = state
    row_count = numerators.shape[0]
    result = numerators.reshape(row_count, HEADS, HEAD_DIM) / totals.T[:, :, None]
    return result.reshape(row_count, HEADS * HEAD_DIM).astype(jnp.bfloat16)


def in_band(block_id, starts, counts):
    return (block_id >= starts[0]) & (block_id < starts[0] + counts[0])


def on_device(
    video_q,
    video_k,
    video_v,
    audio_query_rows,
    audio_k,
    audio_v,
    video_start,
    video_count,
    audio_start,
    audio_count,
):
    own_block = lax.axis_index("seq")
    video_state = partial_results(video_q, audio_k, audio_v)
    audio_state = partial_results(audio_query_rows, video_k, video_v)
    offsets = [offset for offset in range(-RADIUS, RADIUS + 1) if offset != 0]
    for offset in offsets:
        far_query, far_key, far_value = shifted((audio_query_rows, audio_k, audio_v), "seq", offset)
        video_state = merge_in(
            video_state,
            partial_results(video_q, far_key, far_value),
            in_band(own_block - offset, video_start, video_count),
        )
        guest_numerators, guest_maxima, guest_totals = partial_results(far_query, video_k, video_v)
        returned = shifted((guest_numerators, guest_maxima, guest_totals), "seq", -offset)
        audio_state = merge_in(
            audio_state, returned, in_band(own_block + offset, audio_start, audio_count)
        )
    return (finish(video_state), finish(audio_state))


def solution(mesh):
    placed = (
        P(("groups", "seq"), None),
        P(("groups", "seq"), None),
        P(("groups", "seq"), None),
        P(("groups", "seq"), None),
        P(("groups", "seq"), None),
        P(("groups", "seq"), None),
        P(("groups", "seq")),
        P(("groups", "seq")),
        P(("groups", "seq")),
        P(("groups", "seq")),
    )
    return jax.shard_map(
        on_device,
        mesh=mesh,
        in_specs=placed,
        out_specs=(P(("groups", "seq"), None), P(("groups", "seq"), None)),
        check_vma=False,
    )
```

profile of v0, /device:TPU:8, one launch (start us, length us, event | category | flops | bytes accessed | tf_op | source)
XLA Modules:
  0.0 126.9 jit_solution(518093130178578047)
XLA Ops:
  0.6 3.4 %collective-permute-start.8 = (bf16[64,1536]{1,0:T(8,128)(2,1)}, bf16[64,1536]{1,0:T(8,128)(2,1)}, u32[]{:S(2)}, u32[]{:S(2)}) collective-permute-start(bf16[64,1536]{1,0:T(8,128)(2,1)} %param.13), channel_id=1, source_target_pairs={{2,0},{3,1},{4,2},{5,3},{6,4},{7,5},{8,6},{9,7},{10,8},{11,9},{12,... | collective-permute-start | bytes 589832 | tf_op jit(solution)/shard_map/ppermute | solution.py:16
  4.1 1.9 %collective-permute-start.11 = (bf16[64,1536]{1,0:T(8,128)(2,1)}, bf16[64,1536]{1,0:T(8,128)(2,1)}, u32[]{:S(2)}, u32[]{:S(2)}) collective-permute-start(bf16[64,1536]{1,0:T(8,128)(2,1)} %param.13), channel_id=1, source_target_pairs={{1,0},{2,1},{3,2},{4,3},{5,4},{6,5},{7,6},{8,7},{9,8},{10,9},{11,1... | collective-permute-start | bytes 589832 | tf_op jit(solution)/shard_map/ppermute | solution.py:16
  6.0 2.4 %collective-permute-start.14 = (bf16[64,1536]{1,0:T(8,128)(2,1)}, bf16[64,1536]{1,0:T(8,128)(2,1)}, u32[]{:S(2)}, u32[]{:S(2)}) collective-permute-start(bf16[64,1536]{1,0:T(8,128)(2,1)} %param.13), channel_id=1, source_target_pairs={{0,1},{1,2},{2,3},{3,4},{4,5},{5,6},{6,7},{7,8},{8,9},{9,10},{10,1... | collective-permute-start | bytes 589832 | tf_op jit(solution)/shard_map/ppermute | solution.py:16
  8.4 2.6 %collective-permute-start.17 = (bf16[64,1536]{1,0:T(8,128)(2,1)}, bf16[64,1536]{1,0:T(8,128)(2,1)}, u32[]{:S(2)}, u32[]{:S(2)}) collective-permute-start(bf16[64,1536]{1,0:T(8,128)(2,1)} %param.13), channel_id=1, source_target_pairs={{0,2},{1,3},{2,4},{3,5},{4,6},{5,7},{6,8},{7,9},{8,10},{9,11},{10,... | collective-permute-start | bytes 589832 | tf_op jit(solution)/shard_map/ppermute | solution.py:16
  11.0 3.6 %collective-permute-start.4 = (bf16[64,1536]{1,0:T(8,128)(2,1)}, bf16[64,1536]{1,0:T(8,128)(2,1)}, u32[]{:S(2)}, u32[]{:S(2)}) collective-permute-start(bf16[64,1536]{1,0:T(8,128)(2,1)} %param.14), channel_id=1, source_target_pairs={{0,1},{1,2},{2,3},{3,4},{4,5},{5,6},{6,7},{7,8},{8,9},{9,10},{10,1... | collective-permute-start | bytes 589832 | tf_op jit(solution)/shard_map/ppermute | solution.py:16
  14.6 1.4 %copy.47 = bf16[256,1536]{0,1:T(8,128)(2,1)S(1)} copy(bf16[256,1536]{1,0:T(8,128)(2,1)} %param.11) | data formatting | bytes 1572864 | tf_op args[1]
  16.1 0.3 copy.31
  16.4 0.3 fusion.139
  16.6 0.6 copy-done.5
  17.3 1.6 %fusion.42 = f32[12,256,128]{1,2,0:T(8,128)} fusion(f32[12,256,64]{1,2,0:T(8,128)S(1)} %get-tuple-element.33, f32[12,256]{1,0:T(8,128)S(1)} %get-tuple-element.32, bf16[64,1536]{1,0:T(8,128)(2,1)S(1)} %copy-done.5), kind=kOutput, calls=%fused_computation.63 | convolution fusion | flops 50724864 | bytes 2568192 | tf_op jit(solution)/shard_map/hqk,khd->qhd/dot_general | solution.py:32
  18.8 1.8 %fusion.142 = (f32[12,64]{1,0:T(8,128)}, f32[12,64,256]{2,1,0:T(8,128)}) fusion(bf16[256,12,128]{0,2,1:T(8,128)(2,1)S(1)} %bitcast.401, bf16[64,1536]{1,0:T(8,128)(2,1)S(1)} %copy-done.4), kind=kOutput, calls=%fused_computation.187 | convolution fusion | flops 50724096 | bytes 1772544 | tf_op jit(solution)/shard_map/qhd,khd->hqk/dot_general | solution.py:25
  23.2 1.4 %copy.50 = bf16[256,1536]{0,1:T(8,128)(2,1)S(1)} copy(bf16[256,1536]{1,0:T(8,128)(2,1)} %param.12) | data formatting | bytes 1572864 | tf_op args[2]
  24.7 2.1 %fusion.20 = f32[12,64]{1,0:T(8,128)} fusion(f32[12,64,256]{2,1,0:T(8,128)} %get-tuple-element.39, f32[12,64]{1,0:T(8,128)S(1)} %copy-done.7), kind=kLoop, calls=%fused_computation.50 | loop fusion | flops 392448 | bytes 792576 | tf_op jit(solution)/shard_map/reduce_sum | solution.py:30
  26.8 2.9 %collective-permute-start.2 = (bf16[64,1536]{1,0:T(8,128)(2,1)S(1)}, bf16[64,1536]{1,0:T(8,128)(2,1)S(1)}, u32[]{:S(2)}, u32[]{:S(2)}) collective-permute-start(bf16[64,1536]{1,0:T(8,128)(2,1)S(1)} %copy-done.3), channel_id=1, source_target_pairs={{1,0},{2,1},{3,2},{4,3},{5,4},{6,5},{7,6},{8,7},{9,8},{10,9},{11,1... | collective-permute-start | bytes 589832 | tf_op jit(solution)/shard_map/ppermute | solution.py:16
  29.6 1.3 fusion.141
  30.9 3.4 %collective-permute-start = (bf16[64,1536]{1,0:T(8,128)(2,1)S(1)}, bf16[64,1536]{1,0:T(8,128)(2,1)S(1)}, u32[]{:S(2)}, u32[]{:S(2)}) collective-permute-start(bf16[64,1536]{1,0:T(8,128)(2,1)S(1)} %copy-done.3), channel_id=1, source_target_pairs={{2,0},{3,1},{4,2},{5,3},{6,4},{7,5},{8,6},{9,7},{10,8},{11,9},{12,... | collective-permute-start | bytes 589832 | tf_op jit(solution)/shard_map/ppermute | solution.py:16
  34.3 1.9 %fusion.144 = (f32[12,64]{1,0:T(8,128)}, f32[12,64,256]{2,1,0:T(8,128)S(1)}) fusion(bf16[256,12,128]{0,2,1:T(8,128)(2,1)S(1)} %bitcast.403, bf16[64,1536]{1,0:T(8,128)(2,1)} %collective-permute-done.11), kind=kOutput, calls=%fused_computation.189 | convolution fusion | flops 50724096 | bytes 1772544 | tf_op jit(solution)/shard_map/qhd,khd->hqk/dot_general | solution.py:25
  36.2 2.6 %collective-permute-start.6 = (bf16[64,1536]{1,0:T(8,128)(2,1)S(1)}, bf16[64,1536]{1,0:T(8,128)(2,1)S(1)}, u32[]{:S(2)}, u32[]{:S(2)}) collective-permute-start(bf16[64,1536]{1,0:T(8,128)(2,1)S(1)} %copy-done.3), channel_id=1, source_target_pairs={{0,2},{1,3},{2,4},{3,5},{4,6},{5,7},{6,8},{7,9},{8,10},{9,11},{10,... | collective-permute-start | bytes 589832 | tf_op jit(solution)/shard_map/ppermute | solution.py:16
  38.8 1.9 %fusion.145 = (f32[12,64]{1,0:T(8,128)}, f32[12,64,256]{2,1,0:T(8,128)S(1)}) fusion(bf16[256,12,128]{0,2,1:T(8,128)(2,1)S(1)} %bitcast.404, bf16[64,1536]{1,0:T(8,128)(2,1)} %collective-permute-done.14), kind=kOutput, calls=%fused_computation.190 | convolution fusion | flops 50724096 | bytes 1772544 | tf_op jit(solution)/shard_map/qhd,khd->hqk/dot_general | solution.py:25
  40.6 2.4 %collective-permute-start.3 = (bf16[64,1536]{1,0:T(8,128)(2,1)S(1)}, bf16[64,1536]{1,0:T(8,128)(2,1)S(1)}, u32[]{:S(2)}, u32[]{:S(2)}) collective-permute-start(bf16[64,1536]{1,0:T(8,128)(2,1)S(1)} %copy-done.6), channel_id=1, source_target_pairs={{1,0},{2,1},{3,2},{4,3},{5,4},{6,5},{7,6},{8,7},{9,8},{10,9},{11,1... | collective-permute-start | bytes 589832 | tf_op jit(solution)/shard_map/ppermute | solution.py:16
  43.1 1.2 fusion.136
  44.3 3.6 %collective-permute-start.1 = (bf16[64,1536]{1,0:T(8,128)(2,1)S(1)}, bf16[64,1536]{1,0:T(8,128)(2,1)S(1)}, u32[]{:S(2)}, u32[]{:S(2)}) collective-permute-start(bf16[64,1536]{1,0:T(8,128)(2,1)S(1)} %copy-done.6), channel_id=1, source_target_pairs={{2,0},{3,1},{4,2},{5,3},{6,4},{7,5},{8,6},{9,7},{10,8},{11,9},{12,... | collective-permute-start | bytes 589832 | tf_op jit(solution)/shard_map/ppermute | solution.py:16
  47.9 0.3 fusion.137
  48.2 2.1 %collective-permute-start.5 = (bf16[64,1536]{1,0:T(8,128)(2,1)S(1)}, bf16[64,1536]{1,0:T(8,128)(2,1)S(1)}, u32[]{:S(2)}, u32[]{:S(2)}) collective-permute-start(bf16[64,1536]{1,0:T(8,128)(2,1)S(1)} %copy-done.6), channel_id=1, source_target_pairs={{0,1},{1,2},{2,3},{3,4},{4,5},{5,6},{6,7},{7,8},{8,9},{9,10},{10,1... | collective-permute-start | bytes 589832 | tf_op jit(solution)/shard_map/ppermute | solution.py:16
  50.4 0.3 fusion.138
  50.6 0.3 fusion.10
  50.9 2.3 %collective-permute-start.7 = (bf16[64,1536]{1,0:T(8,128)(2,1)S(1)}, bf16[64,1536]{1,0:T(8,128)(2,1)S(1)}, u32[]{:S(2)}, u32[]{:S(2)}) collective-permute-start(bf16[64,1536]{1,0:T(8,128)(2,1)S(1)} %copy-done.6), channel_id=1, source_target_pairs={{0,2},{1,3},{2,4},{3,5},{4,6},{5,7},{6,8},{7,9},{8,10},{9,11},{10,... | collective-permute-start | bytes 589832 | tf_op jit(solution)/shard_map/ppermute | solution.py:16
  53.3 0.3 fusion.140
  53.5 0.1 fusion.18
  53.7 0.3 fusion.14
  54.0 4.0 %collective-permute-start.15 = (f32[12,64]{1,0:T(8,128)}, f32[12,64]{1,0:T(8,128)}, u32[]{:S(2)}, u32[]{:S(2)}) collective-permute-start(f32[12,64]{1,0:T(8,128)} %get-tuple-element.44), channel_id=1, source_target_pairs={{1,0},{2,1},{3,2},{4,3},{5,4},{6,5},{7,6},{8,7},{9,8},{10,9},{11,1... | collective-permute-start | bytes 9224 | tf_op jit(solution)/shard_map/ppermute | solution.py:16
  58.0 1.3 fusion.143
  59.3 1.1 convolution_bitcast_fusion.1
  60.4 3.7 %collective-permute-start.9 = (f32[12,64]{1,0:T(8,128)S(1)}, f32[12,64]{1,0:T(8,128)}, u32[]{:S(2)}, u32[]{:S(2)}) collective-permute-start(f32[12,64]{1,0:T(8,128)S(1)} %get-tuple-element.36), channel_id=1, source_target_pairs={{0,2},{1,3},{2,4},{3,5},{4,6},{5,7},{6,8},{7,9},{8,10},{9,11},{10,... | collective-permute-start | bytes 9224 | tf_op jit(solution)/shard_map/ppermute | solution.py:16
  64.2 0.4 fusion.38
  64.6 1.6 %fusion.26 = f32[12,64]{1,0:T(8,128)} fusion(f32[12,64,256]{2,1,0:T(8,128)S(1)} %get-tuple-element.45, f32[12,64]{1,0:T(8,128)} %get-tuple-element.44), kind=kLoop, calls=%fused_computation.56 | loop fusion | flops 392448 | bytes 792576 | tf_op jit(solution)/shard_map/reduce_sum | solution.py:30
  66.2 0.4 convolution_bitcast_fusion.3
  66.7 1.9 %collective-permute-start.12 = (f32[12,64]{1,0:T(8,128)}, f32[12,64]{1,0:T(8,128)}, u32[]{:S(2)}, u32[]{:S(2)}) collective-permute-start(f32[12,64]{1,0:T(8,128)} %get-tuple-element.42), channel_id=1, source_target_pairs={{0,1},{1,2},{2,3},{3,4},{4,5},{5,6},{6,7},{7,8},{8,9},{9,10},{10,1... | collective-permute-start | bytes 9224 | tf_op jit(solution)/shard_map/ppermute | solution.py:16
  68.6 0.4 fusion.40
  69.0 0.9 fusion.22
  70.0 1.1 convolution_bitcast_fusion.2
  71.1 3.1 %collective-permute-start.20 = (f32[12,64]{1,0:T(8,128)}, f32[12,64]{1,0:T(8,128)}, u32[]{:S(2)}, u32[]{:S(2)}) collective-permute-start(f32[12,64]{1,0:T(8,128)} %fusion.22), channel_id=1, source_target_pairs={{0,2},{1,3},{2,4},{3,5},{4,6},{5,7},{6,8},{7,9},{8,10},{9,11},{10,... | collective-permute-start | bytes 9224 | tf_op jit(solution)/shard_map/ppermute | solution.py:16
  74.2 0.4 fusion.36
  74.7 1.7 %fusion.24 = f32[12,64]{1,0:T(8,128)} fusion(f32[12,64,256]{2,1,0:T(8,128)S(1)} %get-tuple-element.43, f32[12,64]{1,0:T(8,128)} %get-tuple-element.42), kind=kLoop, calls=%fused_computation.54 | loop fusion | flops 392448 | bytes 792576 | tf_op jit(solution)/shard_map/reduce_sum | solution.py:30
  76.4 0.4 convolution_bitcast_fusion
  76.9 3.6 %collective-permute-start.21 = (f32[12,64]{1,0:T(8,128)}, f32[12,64]{1,0:T(8,128)}, u32[]{:S(2)}, u32[]{:S(2)}) collective-permute-start(f32[12,64]{1,0:T(8,128)} %fusion.24), channel_id=1, source_target_pairs={{0,1},{1,2},{2,3},{3,4},{4,5},{5,6},{6,7},{7,8},{8,9},{9,10},{10,1... | collective-permute-start | bytes 9224 | tf_op jit(solution)/shard_map/ppermute | solution.py:16
  80.4 1.1 fusion.2
  81.5 0.9 fusion.28
  82.5 0.8 copy.213
  83.3 1.2 copy.73
  84.5 2.9 %collective-permute-start.22 = (f32[12,64]{1,0:T(8,128)}, f32[12,64]{1,0:T(8,128)S(1)}, u32[]{:S(2)}, u32[]{:S(2)}) collective-permute-start(f32[12,64]{1,0:T(8,128)} %fusion.26), channel_id=1, source_target_pairs={{1,0},{2,1},{3,2},{4,3},{5,4},{6,5},{7,6},{8,7},{9,8},{10,9},{11,1... | collective-permute-start | bytes 9224 | tf_op jit(solution)/shard_map/ppermute | solution.py:16
  87.4 3.0 %collective-permute-start.23 = (f32[12,64]{1,0:T(8,128)}, f32[12,64]{1,0:T(8,128)S(1)}, u32[]{:S(2)}, u32[]{:S(2)}) collective-permute-start(f32[12,64]{1,0:T(8,128)} %fusion.28), channel_id=1, source_target_pairs={{2,0},{3,1},{4,2},{5,3},{6,4},{7,5},{8,6},{9,7},{10,8},{11,9},{12,... | collective-permute-start | bytes 9224 | tf_op jit(solution)/shard_map/ppermute | solution.py:16
  90.4 0.7 fusion.122
  91.1 2.2 %collective-permute-start.18 = (f32[12,64]{1,0:T(8,128)}, f32[12,64]{1,0:T(8,128)S(1)}, u32[]{:S(2)}, u32[]{:S(2)}) collective-permute-start(f32[12,64]{1,0:T(8,128)} %copy-done.8), channel_id=1, source_target_pairs={{2,0},{3,1},{4,2},{5,3},{6,4},{7,5},{8,6},{9,7},{10,8},{11,9},{12,... | collective-permute-start | bytes 9224 | tf_op jit(solution)/shard_map/ppermute | solution.py:16
  93.4 3.6 %collective-permute-start.10 = (f32[64,1536]{1,0:T(8,128)}, f32[64,1536]{1,0:T(8,128)S(1)}, u32[]{:S(2)}, u32[]{:S(2)}) collective-permute-start(f32[64,1536]{1,0:T(8,128)} %bitcast.420), channel_id=1, source_target_pairs={{0,2},{1,3},{2,4},{3,5},{4,6},{5,7},{6,8},{7,9},{8,10},{9,11},{10,... | collective-permute-start | bytes 1179656 | tf_op jit(solution)/shard_map/ppermute | solution.py:16
  97.0 1.9 %collective-permute-start.13 = (f32[64,1536]{1,0:T(8,128)S(1)}, f32[64,1536]{1,0:T(8,128)S(1)}, u32[]{:S(2)}, u32[]{:S(2)}) collective-permute-start(f32[64,1536]{1,0:T(8,128)S(1)} %bitcast.419), channel_id=1, source_target_pairs={{0,1},{1,2},{2,3},{3,4},{4,5},{5,6},{6,7},{7,8},{8,9},{9,10},{10,1... | collective-permute-start | bytes 1179656 | tf_op jit(solution)/shard_map/ppermute | solution.py:16
  99.0 4.5 %collective-permute-start.16 = (f32[64,1536]{1,0:T(8,128)S(1)}, f32[64,1536]{1,0:T(8,128)S(1)}, u32[]{:S(2)}, u32[]{:S(2)}) collective-permute-start(f32[64,1536]{1,0:T(8,128)S(1)} %bitcast.418), channel_id=1, source_target_pairs={{1,0},{2,1},{3,2},{4,3},{5,4},{6,5},{7,6},{8,7},{9,8},{10,9},{11,1... | collective-permute-start | bytes 1179656 | tf_op jit(solution)/shard_map/ppermute | solution.py:16
  103.5 2.2 %collective-permute-start.19 = (f32[64,1536]{1,0:T(8,128)S(1)}, f32[64,1536]{1,0:T(8,128)S(1)}, u32[]{:S(2)}, u32[]{:S(2)}) collective-permute-start(f32[64,1536]{1,0:T(8,128)S(1)} %bitcast.417), channel_id=1, source_target_pairs={{2,0},{3,1},{4,2},{5,3},{6,4},{7,5},{8,6},{9,7},{10,8},{11,9},{12,... | collective-permute-start | bytes 1179656 | tf_op jit(solution)/shard_map/ppermute | solution.py:16
  105.8 0.7 fusion.124
  106.5 0.8 fusion.125
  107.3 12.1 %collective-permute-done.10 = f32[64,1536]{1,0:T(8,128)S(1)} collective-permute-done((f32[64,1536]{1,0:T(8,128)}, f32[64,1536]{1,0:T(8,128)S(1)}, u32[]{:S(2)}, u32[]{:S(2)}) %collective-permute-start.10) | collective-permute-done | bytes 393248 | tf_op jit(solution)/shard_map/ppermute | solution.py:16
  119.4 5.4 %collective-permute-done.19 = f32[64,1536]{1,0:T(8,128)S(1)} collective-permute-done((f32[64,1536]{1,0:T(8,128)S(1)}, f32[64,1536]{1,0:T(8,128)S(1)}, u32[]{:S(2)}, u32[]{:S(2)}) %collective-permute-start.19) | collective-permute-done | bytes 393248 | tf_op jit(solution)/shard_map/ppermute | solution.py:16
  124.8 1.3 %fusion.95 = bf16[12,8,8,128]{3,2,1,0:T(8,128)(2,1)S(1)} fusion(f32[64,12]{0,1:T(8,128)S(1)} %get-tuple-element.20, f32[64,12]{0,1:T(8,128)S(1)} %get-tuple-element.25, f32[64,12]{0,1:T(8,128)S(1)} %get-tuple-element.24, f32[64,12]{0,1:T(8,128)S(1)} %get-tuple-element.21, f32[64,12]{0,1:T(8,128)S(1)} %get-tuple-element.8, ...), kind=kOutput, calls=%fused_computation.122 | convolution fusion | flops 52101120 | bytes 3373056 | tf_op jit(solution)/shard_map/hqk,khd->qhd/dot_general | solution.py:32
  126.2 0.7 copy.214
  (43 shorter events, 0.2 us)
Async XLA Ops:
  0.6 15.7 %copy-start.3 = (bf16[64,1536]{1,0:T(8,128)(2,1)S(1)}, bf16[64,1536]{1,0:T(8,128)(2,1)}, u32[]{:S(2)}) copy-start(bf16[64,1536]{1,0:T(8,128)(2,1)} %param.14) | copy-start | bytes 589828
  0.6 15.4 %copy-start.2 = (bf16[256,1536]{1,0:T(8,128)(2,1)S(1)}, bf16[256,1536]{1,0:T(8,128)(2,1)}, u32[]{:S(2)}) copy-start(bf16[256,1536]{1,0:T(8,128)(2,1)} %param.10) | copy-start | bytes 2359300
  0.6 26.1 %collective-permute-start.8 = (bf16[64,1536]{1,0:T(8,128)(2,1)}, bf16[64,1536]{1,0:T(8,128)(2,1)}, u32[]{:S(2)}, u32[]{:S(2)}) collective-permute-start(bf16[64,1536]{1,0:T(8,128)(2,1)} %param.13), channel_id=1, source_target_pairs={{2,0},{3,1},{4,2},{5,3},{6,4},{7,5},{8,6},{9,7},{10,8},{11,9},{12,... | collective-permute-start | bytes 589832 | tf_op jit(solution)/shard_map/ppermute | solution.py:16
  4.1 26.8 %collective-permute-start.11 = (bf16[64,1536]{1,0:T(8,128)(2,1)}, bf16[64,1536]{1,0:T(8,128)(2,1)}, u32[]{:S(2)}, u32[]{:S(2)}) collective-permute-start(bf16[64,1536]{1,0:T(8,128)(2,1)} %param.13), channel_id=1, source_target_pairs={{1,0},{2,1},{3,2},{4,3},{5,4},{6,5},{7,6},{8,7},{9,8},{10,9},{11,1... | collective-permute-start | bytes 589832 | tf_op jit(solution)/shard_map/ppermute | solution.py:16
  6.0 30.2 %collective-permute-start.14 = (bf16[64,1536]{1,0:T(8,128)(2,1)}, bf16[64,1536]{1,0:T(8,128)(2,1)}, u32[]{:S(2)}, u32[]{:S(2)}) collective-permute-start(bf16[64,1536]{1,0:T(8,128)(2,1)} %param.13), channel_id=1, source_target_pairs={{0,1},{1,2},{2,3},{3,4},{4,5},{5,6},{6,7},{7,8},{8,9},{9,10},{10,1... | collective-permute-start | bytes 589832 | tf_op jit(solution)/shard_map/ppermute | solution.py:16
  8.4 45.5 %collective-permute-start.17 = (bf16[64,1536]{1,0:T(8,128)(2,1)}, bf16[64,1536]{1,0:T(8,128)(2,1)}, u32[]{:S(2)}, u32[]{:S(2)}) collective-permute-start(bf16[64,1536]{1,0:T(8,128)(2,1)} %param.13), channel_id=1, source_target_pairs={{0,2},{1,3},{2,4},{3,5},{4,6},{5,7},{6,8},{7,9},{8,10},{9,11},{10,... | collective-permute-start | bytes 589832 | tf_op jit(solution)/shard_map/ppermute | solution.py:16
  11.0 29.6 %collective-permute-start.4 = (bf16[64,1536]{1,0:T(8,128)(2,1)}, bf16[64,1536]{1,0:T(8,128)(2,1)}, u32[]{:S(2)}, u32[]{:S(2)}) collective-permute-start(bf16[64,1536]{1,0:T(8,128)(2,1)} %param.14), channel_id=1, source_target_pairs={{0,1},{1,2},{2,3},{3,4},{4,5},{5,6},{6,7},{7,8},{8,9},{9,10},{10,1... | collective-permute-start | bytes 589832 | tf_op jit(solution)/shard_map/ppermute | solution.py:16
  16.3 0.9 copy-start.5
  16.6 2.2 %copy-start.4 = (bf16[64,1536]{1,0:T(8,128)(2,1)S(1)}, bf16[64,1536]{1,0:T(8,128)(2,1)}, u32[]{:S(2)}) copy-start(bf16[64,1536]{1,0:T(8,128)(2,1)} %param.13) | copy-start | bytes 589828
  20.6 4.1 %copy-start.7 = (f32[12,64]{1,0:T(8,128)S(1)}, f32[12,64]{1,0:T(8,128)}, u32[]{:S(2)}) copy-start(f32[12,64]{1,0:T(8,128)} %get-tuple-element.38) | copy-start | bytes 9220
  26.8 17.5 %collective-permute-start.2 = (bf16[64,1536]{1,0:T(8,128)(2,1)S(1)}, bf16[64,1536]{1,0:T(8,128)(2,1)S(1)}, u32[]{:S(2)}, u32[]{:S(2)}) collective-permute-start(bf16[64,1536]{1,0:T(8,128)(2,1)S(1)} %copy-done.3), channel_id=1, source_target_pairs={{1,0},{2,1},{3,2},{4,3},{5,4},{6,5},{7,6},{8,7},{9,8},{10,9},{11,1... | collective-permute-start | bytes 589832 | tf_op jit(solution)/shard_map/ppermute | solution.py:16
  30.9 9.7 %copy-start.6 = (bf16[64,1536]{1,0:T(8,128)(2,1)S(1)}, bf16[64,1536]{1,0:T(8,128)(2,1)}, u32[]{:S(2)}) copy-start(bf16[64,1536]{1,0:T(8,128)(2,1)} %param.15) | copy-start | bytes 589828
  30.9 17.3 %collective-permute-start = (bf16[64,1536]{1,0:T(8,128)(2,1)S(1)}, bf16[64,1536]{1,0:T(8,128)(2,1)S(1)}, u32[]{:S(2)}, u32[]{:S(2)}) collective-permute-start(bf16[64,1536]{1,0:T(8,128)(2,1)S(1)} %copy-done.3), channel_id=1, source_target_pairs={{2,0},{3,1},{4,2},{5,3},{6,4},{7,5},{8,6},{9,7},{10,8},{11,9},{12,... | collective-permute-start | bytes 589832 | tf_op jit(solution)/shard_map/ppermute | solution.py:16
  36.2 14.7 %collective-permute-start.6 = (bf16[64,1536]{1,0:T(8,128)(2,1)S(1)}, bf16[64,1536]{1,0:T(8,128)(2,1)S(1)}, u32[]{:S(2)}, u32[]{:S(2)}) collective-permute-start(bf16[64,1536]{1,0:T(8,128)(2,1)S(1)} %copy-done.3), channel_id=1, source_target_pairs={{0,2},{1,3},{2,4},{3,5},{4,6},{5,7},{6,8},{7,9},{8,10},{9,11},{10,... | collective-permute-start | bytes 589832 | tf_op jit(solution)/shard_map/ppermute | solution.py:16
  40.6 19.8 %collective-permute-start.3 = (bf16[64,1536]{1,0:T(8,128)(2,1)S(1)}, bf16[64,1536]{1,0:T(8,128)(2,1)S(1)}, u32[]{:S(2)}, u32[]{:S(2)}) collective-permute-start(bf16[64,1536]{1,0:T(8,128)(2,1)S(1)} %copy-done.6), channel_id=1, source_target_pairs={{1,0},{2,1},{3,2},{4,3},{5,4},{6,5},{7,6},{8,7},{9,8},{10,9},{11,1... | collective-permute-start | bytes 589832 | tf_op jit(solution)/shard_map/ppermute | solution.py:16
  44.3 22.3 %collective-permute-start.1 = (bf16[64,1536]{1,0:T(8,128)(2,1)S(1)}, bf16[64,1536]{1,0:T(8,128)(2,1)S(1)}, u32[]{:S(2)}, u32[]{:S(2)}) collective-permute-start(bf16[64,1536]{1,0:T(8,128)(2,1)S(1)} %copy-done.6), channel_id=1, source_target_pairs={{2,0},{3,1},{4,2},{5,3},{6,4},{7,5},{8,6},{9,7},{10,8},{11,9},{12,... | collective-permute-start | bytes 589832 | tf_op jit(solution)/shard_map/ppermute | solution.py:16
  48.2 22.9 %collective-permute-start.5 = (bf16[64,1536]{1,0:T(8,128)(2,1)S(1)}, bf16[64,1536]{1,0:T(8,128)(2,1)S(1)}, u32[]{:S(2)}, u32[]{:S(2)}) collective-permute-start(bf16[64,1536]{1,0:T(8,128)(2,1)S(1)} %copy-done.6), channel_id=1, source_target_pairs={{0,1},{1,2},{2,3},{3,4},{4,5},{5,6},{6,7},{7,8},{8,9},{9,10},{10,1... | collective-permute-start | bytes 589832 | tf_op jit(solution)/shard_map/ppermute | solution.py:16
  50.9 25.9 %collective-permute-start.7 = (bf16[64,1536]{1,0:T(8,128)(2,1)S(1)}, bf16[64,1536]{1,0:T(8,128)(2,1)S(1)}, u32[]{:S(2)}, u32[]{:S(2)}) collective-permute-start(bf16[64,1536]{1,0:T(8,128)(2,1)S(1)} %copy-done.6), channel_id=1, source_target_pairs={{0,2},{1,3},{2,4},{3,5},{4,6},{5,7},{6,8},{7,9},{8,10},{9,11},{10,... | collective-permute-start | bytes 589832 | tf_op jit(solution)/shard_map/ppermute | solution.py:16
  54.0 37.2 %collective-permute-start.15 = (f32[12,64]{1,0:T(8,128)}, f32[12,64]{1,0:T(8,128)}, u32[]{:S(2)}, u32[]{:S(2)}) collective-permute-start(f32[12,64]{1,0:T(8,128)} %get-tuple-element.44), channel_id=1, source_target_pairs={{1,0},{2,1},{3,2},{4,3},{5,4},{6,5},{7,6},{8,7},{9,8},{10,9},{11,1... | collective-permute-start | bytes 9224 | tf_op jit(solution)/shard_map/ppermute | solution.py:16
  59.2 22.3 %copy-start.8 = (f32[12,64]{1,0:T(8,128)}, f32[12,64]{1,0:T(8,128)S(1)}, u32[]{:S(2)}) copy-start(f32[12,64]{1,0:T(8,128)S(1)} %get-tuple-element.40) | copy-start | bytes 9220
  60.4 24.1 %collective-permute-start.9 = (f32[12,64]{1,0:T(8,128)S(1)}, f32[12,64]{1,0:T(8,128)}, u32[]{:S(2)}, u32[]{:S(2)}) collective-permute-start(f32[12,64]{1,0:T(8,128)S(1)} %get-tuple-element.36), channel_id=1, source_target_pairs={{0,2},{1,3},{2,4},{3,5},{4,6},{5,7},{6,8},{7,9},{8,10},{9,11},{10,... | collective-permute-start | bytes 9224 | tf_op jit(solution)/shard_map/ppermute | solution.py:16
  66.7 20.7 %collective-permute-start.12 = (f32[12,64]{1,0:T(8,128)}, f32[12,64]{1,0:T(8,128)}, u32[]{:S(2)}, u32[]{:S(2)}) collective-permute-start(f32[12,64]{1,0:T(8,128)} %get-tuple-element.42), channel_id=1, source_target_pairs={{0,1},{1,2},{2,3},{3,4},{4,5},{5,6},{6,7},{7,8},{8,9},{9,10},{10,1... | collective-permute-start | bytes 9224 | tf_op jit(solution)/shard_map/ppermute | solution.py:16
  71.1 22.3 %collective-permute-start.20 = (f32[12,64]{1,0:T(8,128)}, f32[12,64]{1,0:T(8,128)}, u32[]{:S(2)}, u32[]{:S(2)}) collective-permute-start(f32[12,64]{1,0:T(8,128)} %fusion.22), channel_id=1, source_target_pairs={{0,2},{1,3},{2,4},{3,5},{4,6},{5,7},{6,8},{7,9},{8,10},{9,11},{10,... | collective-permute-start | bytes 9224 | tf_op jit(solution)/shard_map/ppermute | solution.py:16
  74.7 5.8 %copy-start.1 = (f32[12,256,128]{1,2,0:T(8,128)S(1)}, f32[12,256,128]{1,2,0:T(8,128)}, u32[]{:S(2)}) copy-start(f32[12,256,128]{1,2,0:T(8,128)} %fusion.42) | copy-start | bytes 4718596
  76.9 20.1 %collective-permute-start.21 = (f32[12,64]{1,0:T(8,128)}, f32[12,64]{1,0:T(8,128)}, u32[]{:S(2)}, u32[]{:S(2)}) collective-permute-start(f32[12,64]{1,0:T(8,128)} %fusion.24), channel_id=1, source_target_pairs={{0,1},{1,2},{2,3},{3,4},{4,5},{5,6},{6,7},{7,8},{8,9},{9,10},{10,1... | collective-permute-start | bytes 9224 | tf_op jit(solution)/shard_map/ppermute | solution.py:16
  83.2 41.6 %copy-start = (f32[12,64,256]{2,1,0:T(8,128)S(1)}, f32[12,64,256]{2,1,0:T(8,128)}, u32[]{:S(2)}) copy-start(f32[12,64,256]{2,1,0:T(8,128)} %get-tuple-element.39) | copy-start | bytes 2359300
  84.5 14.5 %collective-permute-start.22 = (f32[12,64]{1,0:T(8,128)}, f32[12,64]{1,0:T(8,128)S(1)}, u32[]{:S(2)}, u32[]{:S(2)}) collective-permute-start(f32[12,64]{1,0:T(8,128)} %fusion.26), channel_id=1, source_target_pairs={{1,0},{2,1},{3,2},{4,3},{5,4},{6,5},{7,6},{8,7},{9,8},{10,9},{11,1... | collective-permute-start | bytes 9224 | tf_op jit(solution)/shard_map/ppermute | solution.py:16
  87.4 16.1 %collective-permute-start.23 = (f32[12,64]{1,0:T(8,128)}, f32[12,64]{1,0:T(8,128)S(1)}, u32[]{:S(2)}, u32[]{:S(2)}) collective-permute-start(f32[12,64]{1,0:T(8,128)} %fusion.28), channel_id=1, source_target_pairs={{2,0},{3,1},{4,2},{5,3},{6,4},{7,5},{8,6},{9,7},{10,8},{11,9},{12,... | collective-permute-start | bytes 9224 | tf_op jit(solution)/shard_map/ppermute | solution.py:16
  91.1 15.4 %collective-permute-start.18 = (f32[12,64]{1,0:T(8,128)}, f32[12,64]{1,0:T(8,128)S(1)}, u32[]{:S(2)}, u32[]{:S(2)}) collective-permute-start(f32[12,64]{1,0:T(8,128)} %copy-done.8), channel_id=1, source_target_pairs={{2,0},{3,1},{4,2},{5,3},{6,4},{7,5},{8,6},{9,7},{10,8},{11,9},{12,... | collective-permute-start | bytes 9224 | tf_op jit(solution)/shard_map/ppermute | solution.py:16
  93.4 26.1 %collective-permute-start.10 = (f32[64,1536]{1,0:T(8,128)}, f32[64,1536]{1,0:T(8,128)S(1)}, u32[]{:S(2)}, u32[]{:S(2)}) collective-permute-start(f32[64,1536]{1,0:T(8,128)} %bitcast.420), channel_id=1, source_target_pairs={{0,2},{1,3},{2,4},{3,5},{4,6},{5,7},{6,8},{7,9},{8,10},{9,11},{10,... | collective-permute-start | bytes 1179656 | tf_op jit(solution)/shard_map/ppermute | solution.py:16
  97.0 22.4 %collective-permute-start.13 = (f32[64,1536]{1,0:T(8,128)S(1)}, f32[64,1536]{1,0:T(8,128)S(1)}, u32[]{:S(2)}, u32[]{:S(2)}) collective-permute-start(f32[64,1536]{1,0:T(8,128)S(1)} %bitcast.419), channel_id=1, source_target_pairs={{0,1},{1,2},{2,3},{3,4},{4,5},{5,6},{6,7},{7,8},{8,9},{9,10},{10,1... | collective-permute-start | bytes 1179656 | tf_op jit(solution)/shard_map/ppermute | solution.py:16
  99.0 20.5 %collective-permute-start.16 = (f32[64,1536]{1,0:T(8,128)S(1)}, f32[64,1536]{1,0:T(8,128)S(1)}, u32[]{:S(2)}, u32[]{:S(2)}) collective-permute-start(f32[64,1536]{1,0:T(8,128)S(1)} %bitcast.418), channel_id=1, source_target_pairs={{1,0},{2,1},{3,2},{4,3},{5,4},{6,5},{7,6},{8,7},{9,8},{10,9},{11,1... | collective-permute-start | bytes 1179656 | tf_op jit(solution)/shard_map/ppermute | solution.py:16
  103.5 21.3 %collective-permute-start.19 = (f32[64,1536]{1,0:T(8,128)S(1)}, f32[64,1536]{1,0:T(8,128)S(1)}, u32[]{:S(2)}, u32[]{:S(2)}) collective-permute-start(f32[64,1536]{1,0:T(8,128)S(1)} %bitcast.417), channel_id=1, source_target_pairs={{2,0},{3,1},{4,2},{5,3},{6,4},{7,5},{8,6},{9,7},{10,8},{11,9},{12,... | collective-permute-start | bytes 1179656 | tf_op jit(solution)/shard_map/ppermute | solution.py:16
where the time goes:
time: 128 us; the launch traced here: 127 us
  starting transfers between devices  70 us (55%)
  matrix products  18.6 us (15%)
  waiting for transfers between devices  17.6 us (14%)
  other arithmetic  10.3 us (8%)
  local copies, waits for them, and re-layouts  6.45 us (5%)
  between operations  3.92 us (3%)
    ppermute x24, starting transfers between devices, shifted(): return lax.ppermute(shard, axis, pairs)  70 us
    ppermute x24, waiting for transfers between devices, shifted(): return lax.ppermute(shard, axis, pairs)  17.6 us
    dot_general x10, matrix products, partial_results(): jnp.einsum('qhd,khd->hqk', query_heads, key_heads, preferred_element_type...  10.3 us
    dot_general x10, matrix products, partial_results(): jnp.einsum('hqk,khd->qhd', weights_bf, value_heads, preferred_element_typ...  8.34 us
    reduce_sum x8, other arithmetic, partial_results(): totals = jnp.sum(raised, axis=-1)  8.01 us
    unnamed x22, local copies, waits for them, and re-layouts  4.9 us
  transfers between devices with their start and end apart: 24, of which 2 were waited for; matrix products, arithmetic and copies ran while one was open for 26% of the time, Pallas kernels for 0%

commit v1 on v0

v1 whole, which is shorter than its diff:
```python
import functools
import math

import jax
import jax.numpy as jnp
from jax import lax
from jax.experimental import pallas as pl
from jax.experimental.pallas import tpu as pltpu
from jax.sharding import PartitionSpec as P

HEAD_DIM = 128
SCALE = math.log2(math.e) / math.sqrt(HEAD_DIM)
NEG = -1e30
BIG = 1e30

VMEM = pl.BlockSpec(memory_space=pltpu.VMEM)
SMEM = pl.BlockSpec(memory_space=pltpu.SMEM)


def pairs_of(n, to):
    pairs = [(s, to(s)) for s in range(n)]
    return [(s, d) for s, d in pairs if d is not None and 0 <= d < n]


def head_cols(h):
    return pl.ds(h * HEAD_DIM, HEAD_DIM)


def nt(a, b):
    return lax.dot_general(a, b, (((1,), (1,)), ((), ())), preferred_element_type=jnp.float32)


def nn(a, b):
    return lax.dot_general(a, b, (((1,), (0,)), ((), ())), preferred_element_type=jnp.float32)


def band_has(block, start, count):
    return (block >= start) & (block < start + count)


def lanes(shape):
    return lax.broadcasted_iota(jnp.int32, shape, len(shape) - 1)


def split3(x):
    hi = x.astype(jnp.bfloat16)
    rest = x - hi.astype(jnp.float32)
    mid = rest.astype(jnp.bfloat16)
    low = (rest - mid.astype(jnp.float32)).astype(jnp.bfloat16)
    return hi, mid, low


def guest_rows(q, k0, k1, v0, v1, in0, in1):
    s0, s1 = nt(q, k0), nt(q, k1)
    m0 = jnp.max(s0, axis=-1, keepdims=True) * SCALE
    m1 = jnp.max(s1, axis=-1, keepdims=True) * SCALE
    m = jnp.maximum(jnp.where(in0, m0, NEG), jnp.where(in1, m1, NEG))
    p0 = jnp.exp2(s0 * SCALE - jnp.where(in0, m, BIG))
    p1 = jnp.exp2(s1 * SCALE - jnp.where(in1, m, BIG))
    total = jnp.sum(p0, axis=-1, keepdims=True) + jnp.sum(p1, axis=-1, keepdims=True)
    total = jnp.maximum(total, 1.0)
    out = nn(p0.astype(jnp.bfloat16), v0) + nn(p1.astype(jnp.bfloat16), v1)
    return out / total, m + jnp.log2(total)


def store_guest(ret, base, heads, outs, stats):
    rows = ret.shape[0]
    lane = lanes((rows, HEAD_DIM))
    packed = jnp.zeros((rows, HEAD_DIM), jnp.float32)
    for h, st in enumerate(stats):
        for piece, val in enumerate(split3(st)):
            packed = jnp.where(lane == piece * 32 + h, val.astype(jnp.float32), packed)
    ret[:, pl.ds(heads * HEAD_DIM, HEAD_DIM)] = packed.astype(jnp.bfloat16)


def guests_kernel(heads, n, two, me, *refs):
    if two:
        start, count, code, qo, qx, k0, k1, v0, v1, own, own_stats, ret = refs
    else:
        code, qx, k0, k1, v0, v1, ret = refs
    me = me[0]
    mate = me ^ 1
    g_start, g_count = code[0] // 8, code[0] % 8
    rows = qx.shape[0]
    total_rows = 2 * rows if two else rows
    if two:
        first = lax.broadcasted_iota(jnp.int32, (total_rows, 1), 0) < rows
        lo = jnp.where(first, start[0], g_start)
        hi = lo + jnp.where(first, count[0], g_count)
    else:
        lo = jnp.full((total_rows, 1), g_start, jnp.int32)
        hi = lo + g_count
    in0 = (lo <= me) & (me < hi)
    in1 = (lo <= mate) & (mate < hi)
    stats = []
    lane = lanes((rows, HEAD_DIM))
    kept = jnp.zeros((rows, HEAD_DIM), jnp.float32)
    for h in range(heads):
        c = head_cols(h)
        q = jnp.concatenate([qo[:, c], qx[:, c]], axis=0) if two else qx[:, c]
        out, lse = guest_rows(q, k0[:, c], k1[:, c], v0[:, c], v1[:, c], in0, in1)
        if two:
            own[:, c] = out[:rows]
            kept = jnp.where(lane == h, lse[:rows], kept)
            out, lse = out[rows:], lse[rows:]
        ret[:, c] = out.astype(jnp.bfloat16)
        stats.append(lse)
    if two:
        own_stats[...] = kept
    store_guest(ret, 0, heads, None, stats)


def audio_kernel(heads, me, start, count, own, own_stats, rx, rz, out):
    me = me[0]
    chip = me // 2
    step = 1 - 2 * (chip % 2)
    cx, cz = chip + step, chip - step
    lo, hi = start[0], start[0] + count[0]

    def reaches(c):
        return (2 * c < hi) & (2 * c + 2 > lo)

    tail = pl.ds(heads * HEAD_DIM, HEAD_DIM)
    sx, sz = rx[:, tail].astype(jnp.float32), rz[:, tail].astype(jnp.float32)
    ok_x, ok_z = reaches(cx), reaches(cz)
    for h in range(heads):
        c = head_cols(h)

        def lse_of(st, ok):
            v = st[:, h : h + 1] + st[:, 32 + h : 33 + h] + st[:, 64 + h : 65 + h]
            return jnp.where(ok, v, NEG)

        l0 = own_stats[:, h : h + 1]
        l1, l2 = lse_of(sx, ok_x), lse_of(sz, ok_z)
        m = jnp.maximum(l0, jnp.maximum(l1, l2))
        w0, w1, w2 = jnp.exp2(l0 - m), jnp.exp2(l1 - m), jnp.exp2(l2 - m)
        r = 1.0 / (w0 + w1 + w2)
        acc = own[:, c] * (w0 * r)
        acc = acc + rx[:, c].astype(jnp.float32) * (w1 * r)
        acc = acc + rz[:, c].astype(jnp.float32) * (w2 * r)
        out[:, c] = acc.astype(jnp.bfloat16)


def video_kernel(heads, me, start, count, q, k0, k1, k2, k3, k4, k5, v0, v1, v2, v3, v4, v5, out):
    me = me[0]
    chip, core = me // 2, me % 2
    x = chip % 2
    lo, hi = start[0], start[0] + count[0]
    far = jnp.where(core == 0, me - 1, me + 1)
    zid = jnp.where(x == 0, me - 2, me + 2)
    by_x = x != core
    never = -1000
    ids = [me, me ^ 1, me ^ 2, jnp.where(by_x, far, never), zid, jnp.where(by_x, never, far)]
    keys = k0.shape[0]
    lane = lanes((1, 2 * keys))
    bias = []
    for j in range(3):
        a, b = ids[2 * j], ids[2 * j + 1]
        block = jnp.where(lane < keys, a, b)
        bias.append(jnp.where((block >= lo) & (block < hi), 0.0, NEG))
    ks, vs = (k0, k1, k2, k3, k4, k5), (v0, v1, v2, v3, v4, v5)
    for h in range(heads):
        c = head_cols(h)
        qh = q[:, c]
        ts = []
        for j in range(3):
            kk = jnp.concatenate([ks[2 * j][:, c], ks[2 * j + 1][:, c]], axis=0)
            ts.append(nt(qh, kk) * SCALE + bias[j])
        m = jnp.max(jnp.maximum(jnp.maximum(ts[0], ts[1]), ts[2]), axis=-1, keepdims=True)
        ps = [jnp.exp2(t - m) for t in ts]
        total = jnp.sum(ps[0] + ps[1] + ps[2], axis=-1, keepdims=True)
        acc = 0.0
        for j in range(3):
            vv = jnp.concatenate([vs[2 * j][:, c], vs[2 * j + 1][:, c]], axis=0)
            acc = acc + nn(ps[j].astype(jnp.bfloat16), vv)
        out[:, c] = (acc / total).astype(jnp.bfloat16)


def call(kernel, outs, n_smem, n_vmem):
    return pl.pallas_call(
        kernel,
        out_shape=outs,
        in_specs=[SMEM] * n_smem + [VMEM] * n_vmem,
        out_specs=jax.tree.map(lambda _: VMEM, outs),
    )


def on_device(n, vq, vk, vv, aq, ak, av, v_start, v_count, a_start, a_count):
    rows, features = aq.shape
    heads = features // HEAD_DIM

    def move(x, pairs):
        return lax.ppermute(x, "seq", pairs)

    across = pairs_of(n, lambda s: s ^ 2)
    mates = pairs_of(n, lambda s: s ^ 1)
    along = pairs_of(n, lambda s: s - 4 if s & 2 else s + 4)
    diagonal = pairs_of(n, lambda s: s + 2 if s & 2 else s - 2)
    far_x = pairs_of(n, lambda s: s ^ 1 if s % 4 in (0, 3) else None)
    far_z = pairs_of(n, lambda s: s ^ 1 if s % 4 in (1, 2) else None)

    me = lax.axis_index("seq").astype(jnp.int32).reshape(1)
    code = a_start * 8 + a_count

    xq = move(aq, across)
    x_code = move(code, across)
    z_code = move(code, diagonal)
    xk = move(ak, across)
    xv = move(av, across)
    mk, mv = move(vk, mates), move(vv, mates)
    pk, pv = move(ak, mates), move(av, mates)
    zq = move(xq, along)

    f32, bf16 = jnp.float32, jnp.bfloat16
    ret_shape = jax.ShapeDtypeStruct((rows, features + HEAD_DIM), bf16)
    own, own_stats, ret_x = call(
        functools.partial(guests_kernel, heads, n, True),
        (
            jax.ShapeDtypeStruct((rows, features), f32),
            jax.ShapeDtypeStruct((rows, HEAD_DIM), f32),
            ret_shape,
        ),
        4,
        6,
    )(me, a_start, a_count, x_code, aq, xq, vk, mk, vv, mv)
    got_x = move(ret_x, across)
    zk = move(xk, along)
    (ret_z,) = call(functools.partial(guests_kernel, heads, n, False), (ret_shape,), 2, 5)(
        me, z_code, zq, vk, mk, vv, mv
    )
    got_z = move(ret_z, diagonal)
    zv = move(xv, along)
    fxk, fxv = move(xk, far_x), move(xv, far_x)
    fzk, fzv = move(zk, far_z), move(zv, far_z)
    (audio,) = call(
        functools.partial(audio_kernel, heads), (jax.ShapeDtypeStruct(aq.shape, bf16),), 3, 4
    )(me, a_start, a_count, own, own_stats, got_x, got_z)
    (video,) = call(
        functools.partial(video_kernel, heads), (jax.ShapeDtypeStruct(vq.shape, bf16),), 3, 13
    )(me, v_start, v_count, vq, ak, pk, xk, fxk, zk, fzk, av, pv, xv, fxv, zv, fzv)
    return video, audio


def solution(mesh):
    rows = P(("groups", "seq"), None)
    each = P(("groups", "seq"))
    return jax.shard_map(
        functools.partial(on_device, mesh.shape["seq"]),
        mesh=mesh,
        in_specs=(rows,) * 6 + (each,) * 4,
        out_specs=(rows, rows),
        check_vma=False,
    )
```

time: 128 us -> 64 us (0.50)
  the two profiles are of different devices: /device:TPU:8 before, /device:TPU:13 now
where the time goes in v1:
time: 64 us; the launch traced here: 63.6 us
  starting transfers between devices  37.4 us (58%)
  Pallas kernels  20.4 us (32%)
  between operations  3.54 us (6%)
  local copies, waits for them, and re-layouts  2.12 us (3%)
    ppermute x18, starting transfers between devices, move(): return lax.ppermute(x, 'seq', pairs)  37.4 us
    pallas_call x1, Pallas kernels, on_device(): call(functools.partial(guests_kernel, heads, n, True), (jax.ShapeDtypeStr...  7 us
    pallas_call x1, Pallas kernels, on_device(): call(functools.partial(guests_kernel, heads, n, False), (ret_shape,), 2, 5)  6.37 us
    pallas_call x1, Pallas kernels, on_device(): call(functools.partial(video_kernel, heads), (jax.ShapeDtypeStruct(vq.sha...  4.71 us
    pallas_call x1, Pallas kernels, on_device(): call(functools.partial(audio_kernel, heads), (jax.ShapeDtypeStruct(aq.sha...  2.35 us
    unnamed x34, local copies, waits for them, and re-layouts  2.12 us
  transfers between devices with their start and end apart: 18, of which 1 were waited for; matrix products, arithmetic and copies ran while one was open for 0% of the time, Pallas kernels for 28%

profile of v1, /device:TPU:13, one launch (start us, length us, event | category | flops | bytes accessed | tf_op | source)
XLA Modules:
  0.0 63.6 jit_solution(13231692666345540210)
XLA Ops:
  0.6 0.7 %collective-permute-start.12 = (bf16[256,1536]{1,0:T(8,128)(2,1)}, bf16[256,1536]{1,0:T(8,128)(2,1)S(1)}, u32[]{:S(2)}, u32[]{:S(2)}) collective-permute-start(bf16[256,1536]{1,0:T(8,128)(2,1)} %refs_2_.1), channel_id=1, source_target_pairs={{0,1},{1,0},{2,3},{3,2},{4,5},{5,4},{6,7},{7,6},{8,9},{9,8},{10,11... | collective-permute-start | bytes 2359304 | tf_op jit(solution)/shard_map/ppermute | solution.py:193
  1.4 0.1 collective-permute-start.13
  1.5 1.2 %collective-permute-start.11 = (bf16[64,1536]{1,0:T(8,128)(2,1)}, bf16[64,1536]{1,0:T(8,128)(2,1)S(1)}, u32[]{:S(2)}, u32[]{:S(2)}) collective-permute-start(bf16[64,1536]{1,0:T(8,128)(2,1)} %refs_3_.1), channel_id=1, source_target_pairs={{0,2},{1,3},{2,0},{3,1},{4,6},{5,7},{6,4},{7,5},{8,10},{9,11},{10,... | collective-permute-start | bytes 589832 | tf_op jit(solution)/shard_map/ppermute | solution.py:193
  4.0 2.8 %collective-permute-start.10 = (s32[1]{0:T(128)}, s32[1]{0:T(128)}, u32[]{:S(2)}, u32[]{:S(2)}) collective-permute-start(s32[1]{0:T(128)} %add.3), channel_id=1, source_target_pairs={{0,2},{1,3},{2,0},{3,1},{4,6},{5,7},{6,4},{7,5},{8,10},{9,11},{10,... | collective-permute-start | bytes 20 | tf_op jit(solution)/shard_map/ppermute | solution.py:193
  6.8 2.7 %collective-permute-start.15 = (s32[1]{0:T(128)}, s32[1]{0:T(128)}, u32[]{:S(2)}, u32[]{:S(2)}) collective-permute-start(s32[1]{0:T(128)} %add.3), channel_id=1, source_target_pairs={{2,4},{3,5},{4,2},{5,3},{6,8},{7,9},{8,6},{9,7},{10,12},{11,13},{1... | collective-permute-start | bytes 20 | tf_op jit(solution)/shard_map/ppermute | solution.py:193
  9.6 2.3 %collective-permute-start.1 = (bf16[64,1536]{1,0:T(8,128)(2,1)}, bf16[64,1536]{1,0:T(8,128)(2,1)S(1)}, u32[]{:S(2)}, u32[]{:S(2)}) collective-permute-start(bf16[64,1536]{1,0:T(8,128)(2,1)} %k0.1), channel_id=1, source_target_pairs={{0,2},{1,3},{2,0},{3,1},{4,6},{5,7},{6,4},{7,5},{8,10},{9,11},{10,... | collective-permute-start | bytes 589832 | tf_op jit(solution)/shard_map/ppermute | solution.py:193
  11.9 0.1 collective-permute-done.15.refs_0_
  12.0 0.3 collective-permute-start.6
  12.2 0.0 collective-permute-done.11.refs_4_
  12.2 3.2 %collective-permute-start.16 = (bf16[64,1536]{1,0:T(8,128)(2,1)S(1)}, bf16[64,1536]{1,0:T(8,128)(2,1)S(1)}, u32[]{:S(2)}, u32[]{:S(2)}) collective-permute-start(bf16[64,1536]{1,0:T(8,128)(2,1)S(1)} %collective-permute-done.11.refs_4_), channel_id=1, source_target_pairs={{0,4},{1,5},{4,8},{5,9},{6,2},{7,3},{8,12},{9,13},{10,6},{11,7},{1... | collective-permute-start | bytes 589832 | tf_op jit(solution)/shard_map/ppermute | solution.py:193
  15.4 0.0 collective-permute-done.1.k2
  15.4 0.0 copy-start.4
  15.4 4.6 %collective-permute-start = (bf16[64,1536]{1,0:T(8,128)(2,1)}, bf16[64,1536]{1,0:T(8,128)(2,1)S(1)}, u32[]{:S(2)}, u32[]{:S(2)}) collective-permute-start(bf16[64,1536]{1,0:T(8,128)(2,1)} %k0.1), channel_id=1, source_target_pairs={{0,1},{1,0},{2,3},{3,2},{4,5},{5,4},{6,7},{7,6},{8,9},{9,8},{10,11... | collective-permute-start | bytes 589832 | tf_op jit(solution)/shard_map/ppermute | solution.py:193
  20.1 0.0 collective-permute-done.6.v2
  20.1 2.1 %collective-permute-start.5 = (bf16[64,1536]{1,0:T(8,128)(2,1)}, bf16[64,1536]{1,0:T(8,128)(2,1)S(1)}, u32[]{:S(2)}, u32[]{:S(2)}) collective-permute-start(bf16[64,1536]{1,0:T(8,128)(2,1)} %v0.1), channel_id=1, source_target_pairs={{0,1},{1,0},{2,3},{3,2},{4,5},{5,4},{6,7},{7,6},{8,9},{9,8},{10,11... | collective-permute-start | bytes 589832 | tf_op jit(solution)/shard_map/ppermute | solution.py:193
  22.2 0.0 collective-permute-done.16.refs_1_
  22.2 3.2 %collective-permute-start.3 = (bf16[64,1536]{1,0:T(8,128)(2,1)S(1)}, bf16[64,1536]{1,0:T(8,128)(2,1)S(1)}, u32[]{:S(2)}, u32[]{:S(2)}) collective-permute-start(bf16[64,1536]{1,0:T(8,128)(2,1)S(1)} %collective-permute-done.1.k2), channel_id=1, source_target_pairs={{0,4},{1,5},{4,8},{5,9},{6,2},{7,3},{8,12},{9,13},{10,6},{11,7},{1... | collective-permute-start | bytes 589832 | tf_op jit(solution)/shard_map/ppermute | solution.py:193
  25.4 0.0 collective-permute-done.12.refs_6_.refs_3_
  25.4 0.0 copy-start
  25.4 2.6 %collective-permute-start.8 = (bf16[64,1536]{1,0:T(8,128)(2,1)S(1)}, bf16[64,1536]{1,0:T(8,128)(2,1)S(1)}, u32[]{:S(2)}, u32[]{:S(2)}) collective-permute-start(bf16[64,1536]{1,0:T(8,128)(2,1)S(1)} %collective-permute-done.6.v2), channel_id=1, source_target_pairs={{0,4},{1,5},{4,8},{5,9},{6,2},{7,3},{8,12},{9,13},{10,6},{11,7},{1... | collective-permute-start | bytes 589832 | tf_op jit(solution)/shard_map/ppermute | solution.py:193
  28.0 0.0 collective-permute-done.13.refs_8_.refs_5_
  28.1 0.0 copy-start.1
  28.1 1.3 %collective-permute-start.2 = (bf16[64,1536]{1,0:T(8,128)(2,1)S(1)}, bf16[64,1536]{1,0:T(8,128)(2,1)S(1)}, u32[]{:S(2)}, u32[]{:S(2)}) collective-permute-start(bf16[64,1536]{1,0:T(8,128)(2,1)S(1)} %collective-permute-done.1.k2), channel_id=1, source_target_pairs={{0,1},{3,2},{4,5},{7,6},{8,9},{11,10},{12,13},{15,14},{16,17},{19,... | collective-permute-start | bytes 589832 | tf_op jit(solution)/shard_map/ppermute | solution.py:193
  29.4 0.0 copy-done.14
  29.4 0.0 copy-done
  29.4 0.0 copy-done.1
  29.4 7.0 %shard_map.114 = (f32[64,1536]{1,0:T(8,128)}, f32[64,128]{1,0:T(8,128)}, bf16[64,1664]{1,0:T(8,128)(2,1)}) custom-call(s32[1]{0:T(128)} %bitcast.me, s32[1]{0:T(128)S(6)} %copy.14.refs_0_.start, s32[1]{0:T(128)S(6)} %copy.15.refs_1_.count, s32[1]{0:T(128)} %collective-permute-done.10.refs_2_, bf16[64,1536]{1,0:T(8,128)(2,1)} %refs_3_.1, ...), custom_call_target="tpu_custom_call" | custom-call | tf_op jit(solution)/shard_map/pallas_call | solution.py:216
  36.4 0.0 copy-done.4
  36.4 0.0 copy-done.15
  36.4 6.4 %shard_map.115 = bf16[64,1664]{1,0:T(8,128)(2,1)} custom-call(s32[1]{0:T(128)} %bitcast.me, s32[1]{0:T(128)} %collective-permute-done.15.refs_0_, bf16[64,1536]{1,0:T(8,128)(2,1)} %copy-done.15, bf16[256,1536]{1,0:T(8,128)(2,1)} %refs_2_.1, bf16[256,1536]{1,0:T(8,128)(2,1)} %copy-done, bf16[256,1536]{1,0:T(8,128)(2,1)} %refs_4_.1, bf16[256,1536]{1,0:T(8,128)(2,1)} %copy-done.1), custom_call_target="tpu_custom_call" | custom-call | tf_op jit(solution)/shard_map/pallas_call | solution.py:228
  42.8 0.0 collective-permute-done.k1
  42.8 0.0 copy-done.16
  42.8 0.6 collective-permute-start.14
  43.4 0.0 collective-permute-done.5.v1
  43.4 3.3 %collective-permute-start.17 = (bf16[64,1664]{1,0:T(8,128)(2,1)}, bf16[64,1664]{1,0:T(8,128)(2,1)S(1)}, u32[]{:S(2)}, u32[]{:S(2)}) collective-permute-start(bf16[64,1664]{1,0:T(8,128)(2,1)} %shard_map.115), channel_id=1, source_target_pairs={{2,4},{3,5},{4,2},{5,3},{6,8},{7,9},{8,6},{9,7},{10,12},{11,13},{1... | collective-permute-start | bytes 638984 | tf_op jit(solution)/shard_map/ppermute | solution.py:193
  46.7 0.0 collective-permute-done.3.k4
  46.7 0.0 copy-done.5
  46.7 0.0 copy-start.8
  46.7 1.3 %collective-permute-start.7 = (bf16[64,1536]{1,0:T(8,128)(2,1)S(1)}, bf16[64,1536]{1,0:T(8,128)(2,1)S(1)}, u32[]{:S(2)}, u32[]{:S(2)}) collective-permute-start(bf16[64,1536]{1,0:T(8,128)(2,1)S(1)} %collective-permute-done.6.v2), channel_id=1, source_target_pairs={{0,1},{3,2},{4,5},{7,6},{8,9},{11,10},{12,13},{15,14},{16,17},{19,... | collective-permute-start | bytes 589832 | tf_op jit(solution)/shard_map/ppermute | solution.py:193
  48.0 0.0 collective-permute-done.8.v4
  48.0 0.0 copy-start.9
  48.1 3.6 %collective-permute-start.4 = (bf16[64,1536]{1,0:T(8,128)(2,1)S(1)}, bf16[64,1536]{1,0:T(8,128)(2,1)S(1)}, u32[]{:S(2)}, u32[]{:S(2)}) collective-permute-start(bf16[64,1536]{1,0:T(8,128)(2,1)S(1)} %collective-permute-done.3.k4), channel_id=1, source_target_pairs={{1,0},{2,3},{5,4},{6,7},{9,8},{10,11},{13,12},{14,15},{17,16},{18,... | collective-permute-start | bytes 589832 | tf_op jit(solution)/shard_map/ppermute | solution.py:193
  51.7 0.0 collective-permute-done.2.k3
  51.7 0.0 copy-start.10
  51.7 1.3 %collective-permute-start.9 = (bf16[64,1536]{1,0:T(8,128)(2,1)S(1)}, bf16[64,1536]{1,0:T(8,128)(2,1)S(1)}, u32[]{:S(2)}, u32[]{:S(2)}) collective-permute-start(bf16[64,1536]{1,0:T(8,128)(2,1)S(1)} %collective-permute-done.8.v4), channel_id=1, source_target_pairs={{1,0},{2,3},{5,4},{6,7},{9,8},{10,11},{13,12},{14,15},{17,16},{18,... | collective-permute-start | bytes 589832 | tf_op jit(solution)/shard_map/ppermute | solution.py:193
  54.3 0.0 collective-permute-done.7.v3
  54.3 0.0 copy-start.11
  54.3 0.0 collective-permute-done.4.k5
  54.3 0.0 copy-start.12
  54.4 0.0 collective-permute-done.9.v5
  54.4 0.0 copy-done.6
  54.4 0.0 copy-done.7
  54.4 0.0 copy-done.8
  54.4 0.0 copy-done.9
  54.4 0.6 copy-done.11
  55.0 0.1 copy-done.12
  55.1 0.7 %copy-done.13 = bf16[64,1536]{1,0:T(8,128)(2,1)} copy-done((bf16[64,1536]{1,0:T(8,128)(2,1)}, bf16[64,1536]{1,0:T(8,128)(2,1)S(1)}, u32[]{:S(2)}) %copy-start.13) | copy-done | bytes 196632
  55.7 4.7 %shard_map.113 = bf16[256,1536]{1,0:T(8,128)(2,1)} custom-call(s32[1]{0:T(128)} %bitcast.me, s32[1]{0:T(128)S(6)} %copy.12.start, s32[1]{0:T(128)S(6)} %copy.13.count, bf16[256,1536]{1,0:T(8,128)(2,1)} %q.1, bf16[64,1536]{1,0:T(8,128)(2,1)} %k0.1, bf16[64,1536]{1,0:T(8,128)(2,1)} %copy-done.6, bf16[64,1536]{1,0:T(8,128)(2,1)} %copy-done.4, ...), custom_call_target="tpu_custom_call" | custom-call | tf_op jit(solution)/shard_map/pallas_call | solution.py:238
  60.4 0.0 collective-permute-done.14.rx
  60.5 0.0 collective-permute-done.17.rz
  60.5 0.0 copy-start.3
  60.5 0.7 %copy-done.2 = bf16[64,1664]{1,0:T(8,128)(2,1)} copy-done((bf16[64,1664]{1,0:T(8,128)(2,1)}, bf16[64,1664]{1,0:T(8,128)(2,1)S(1)}, u32[]{:S(2)}) %copy-start.2) | copy-done | bytes 213016
  61.1 0.1 copy-done.3
  61.2 2.3 %shard_map.116 = bf16[64,1536]{1,0:T(8,128)(2,1)} custom-call(s32[1]{0:T(128)} %bitcast.me, s32[1]{0:T(128)S(6)} %copy.14.refs_0_.start, s32[1]{0:T(128)S(6)} %copy.15.refs_1_.count, f32[64,1536]{1,0:T(8,128)} %get-tuple-element.5.own, f32[64,128]{1,0:T(8,128)} %get-tuple-element.6.own_stats, bf16[64,1664]{1,0:T(8,128)(2,1)} %copy-done.2, ...), custom_call_target="tpu_custom_call" | custom-call | tf_op jit(solution)/shard_map/pallas_call | solution.py:235
  (10 shorter events, 0.0 us)
Async XLA Ops:
  0.6 24.8 %collective-permute-start.12 = (bf16[256,1536]{1,0:T(8,128)(2,1)}, bf16[256,1536]{1,0:T(8,128)(2,1)S(1)}, u32[]{:S(2)}, u32[]{:S(2)}) collective-permute-start(bf16[256,1536]{1,0:T(8,128)(2,1)} %refs_2_.1), channel_id=1, source_target_pairs={{0,1},{1,0},{2,3},{3,2},{4,5},{5,4},{6,7},{7,6},{8,9},{9,8},{10,11... | collective-permute-start | bytes 2359304 | tf_op jit(solution)/shard_map/ppermute | solution.py:193
  1.4 26.7 %collective-permute-start.13 = (bf16[256,1536]{1,0:T(8,128)(2,1)}, bf16[256,1536]{1,0:T(8,128)(2,1)S(1)}, u32[]{:S(2)}, u32[]{:S(2)}) collective-permute-start(bf16[256,1536]{1,0:T(8,128)(2,1)} %refs_4_.1), channel_id=1, source_target_pairs={{0,1},{1,0},{2,3},{3,2},{4,5},{5,4},{6,7},{7,6},{8,9},{9,8},{10,11... | collective-permute-start | bytes 2359304 | tf_op jit(solution)/shard_map/ppermute | solution.py:193
  1.5 10.8 %collective-permute-start.11 = (bf16[64,1536]{1,0:T(8,128)(2,1)}, bf16[64,1536]{1,0:T(8,128)(2,1)S(1)}, u32[]{:S(2)}, u32[]{:S(2)}) collective-permute-start(bf16[64,1536]{1,0:T(8,128)(2,1)} %refs_3_.1), channel_id=1, source_target_pairs={{0,2},{1,3},{2,0},{3,1},{4,6},{5,7},{6,4},{7,5},{8,10},{9,11},{10,... | collective-permute-start | bytes 589832 | tf_op jit(solution)/shard_map/ppermute | solution.py:193
  4.0 5.6 %collective-permute-start.10 = (s32[1]{0:T(128)}, s32[1]{0:T(128)}, u32[]{:S(2)}, u32[]{:S(2)}) collective-permute-start(s32[1]{0:T(128)} %add.3), channel_id=1, source_target_pairs={{0,2},{1,3},{2,0},{3,1},{4,6},{5,7},{6,4},{7,5},{8,10},{9,11},{10,... | collective-permute-start | bytes 20 | tf_op jit(solution)/shard_map/ppermute | solution.py:193
  6.8 5.2 %collective-permute-start.15 = (s32[1]{0:T(128)}, s32[1]{0:T(128)}, u32[]{:S(2)}, u32[]{:S(2)}) collective-permute-start(s32[1]{0:T(128)} %add.3), channel_id=1, source_target_pairs={{2,4},{3,5},{4,2},{5,3},{6,8},{7,9},{8,6},{9,7},{10,12},{11,13},{1... | collective-permute-start | bytes 20 | tf_op jit(solution)/shard_map/ppermute | solution.py:193
  9.6 5.9 %collective-permute-start.1 = (bf16[64,1536]{1,0:T(8,128)(2,1)}, bf16[64,1536]{1,0:T(8,128)(2,1)S(1)}, u32[]{:S(2)}, u32[]{:S(2)}) collective-permute-start(bf16[64,1536]{1,0:T(8,128)(2,1)} %k0.1), channel_id=1, source_target_pairs={{0,2},{1,3},{2,0},{3,1},{4,6},{5,7},{6,4},{7,5},{8,10},{9,11},{10,... | collective-permute-start | bytes 589832 | tf_op jit(solution)/shard_map/ppermute | solution.py:193
  12.0 8.1 %collective-permute-start.6 = (bf16[64,1536]{1,0:T(8,128)(2,1)}, bf16[64,1536]{1,0:T(8,128)(2,1)S(1)}, u32[]{:S(2)}, u32[]{:S(2)}) collective-permute-start(bf16[64,1536]{1,0:T(8,128)(2,1)} %v0.1), channel_id=1, source_target_pairs={{0,2},{1,3},{2,0},{3,1},{4,6},{5,7},{6,4},{7,5},{8,10},{9,11},{10,... | collective-permute-start | bytes 589832 | tf_op jit(solution)/shard_map/ppermute | solution.py:193
  12.2 17.1 %copy-start.14 = (bf16[64,1536]{1,0:T(8,128)(2,1)}, bf16[64,1536]{1,0:T(8,128)(2,1)S(1)}, u32[]{:S(2)}) copy-start(bf16[64,1536]{1,0:T(8,128)(2,1)S(1)} %collective-permute-done.11.refs_4_) | copy-start | bytes 589828
  12.2 10.0 %collective-permute-start.16 = (bf16[64,1536]{1,0:T(8,128)(2,1)S(1)}, bf16[64,1536]{1,0:T(8,128)(2,1)S(1)}, u32[]{:S(2)}, u32[]{:S(2)}) collective-permute-start(bf16[64,1536]{1,0:T(8,128)(2,1)S(1)} %collective-permute-done.11.refs_4_), channel_id=1, source_target_pairs={{0,4},{1,5},{4,8},{5,9},{6,2},{7,3},{8,12},{9,13},{10,6},{11,7},{1... | collective-permute-start | bytes 589832 | tf_op jit(solution)/shard_map/ppermute | solution.py:193
  15.4 21.0 %copy-start.4 = (bf16[64,1536]{1,0:T(8,128)(2,1)}, bf16[64,1536]{1,0:T(8,128)(2,1)S(1)}, u32[]{:S(2)}) copy-start(bf16[64,1536]{1,0:T(8,128)(2,1)S(1)} %collective-permute-done.1.k2) | copy-start | bytes 589828
  15.4 27.3 %collective-permute-start = (bf16[64,1536]{1,0:T(8,128)(2,1)}, bf16[64,1536]{1,0:T(8,128)(2,1)S(1)}, u32[]{:S(2)}, u32[]{:S(2)}) collective-permute-start(bf16[64,1536]{1,0:T(8,128)(2,1)} %k0.1), channel_id=1, source_target_pairs={{0,1},{1,0},{2,3},{3,2},{4,5},{5,4},{6,7},{7,6},{8,9},{9,8},{10,11... | collective-permute-start | bytes 589832 | tf_op jit(solution)/shard_map/ppermute | solution.py:193
  20.1 26.6 %copy-start.5 = (bf16[64,1536]{1,0:T(8,128)(2,1)}, bf16[64,1536]{1,0:T(8,128)(2,1)S(1)}, u32[]{:S(2)}) copy-start(bf16[64,1536]{1,0:T(8,128)(2,1)S(1)} %collective-permute-done.6.v2) | copy-start | bytes 589828
  20.1 23.3 %collective-permute-start.5 = (bf16[64,1536]{1,0:T(8,128)(2,1)}, bf16[64,1536]{1,0:T(8,128)(2,1)S(1)}, u32[]{:S(2)}, u32[]{:S(2)}) collective-permute-start(bf16[64,1536]{1,0:T(8,128)(2,1)} %v0.1), channel_id=1, source_target_pairs={{0,1},{1,0},{2,3},{3,2},{4,5},{5,4},{6,7},{7,6},{8,9},{9,8},{10,11... | collective-permute-start | bytes 589832 | tf_op jit(solution)/shard_map/ppermute | solution.py:193
  22.2 14.2 %copy-start.15 = (bf16[64,1536]{1,0:T(8,128)(2,1)}, bf16[64,1536]{1,0:T(8,128)(2,1)S(1)}, u32[]{:S(2)}) copy-start(bf16[64,1536]{1,0:T(8,128)(2,1)S(1)} %collective-permute-done.16.refs_1_) | copy-start | bytes 589828
  22.2 24.5 %collective-permute-start.3 = (bf16[64,1536]{1,0:T(8,128)(2,1)S(1)}, bf16[64,1536]{1,0:T(8,128)(2,1)S(1)}, u32[]{:S(2)}, u32[]{:S(2)}) collective-permute-start(bf16[64,1536]{1,0:T(8,128)(2,1)S(1)} %collective-permute-done.1.k2), channel_id=1, source_target_pairs={{0,4},{1,5},{4,8},{5,9},{6,2},{7,3},{8,12},{9,13},{10,6},{11,7},{1... | collective-permute-start | bytes 589832 | tf_op jit(solution)/shard_map/ppermute | solution.py:193
  25.4 4.0 %copy-start = (bf16[256,1536]{1,0:T(8,128)(2,1)}, bf16[256,1536]{1,0:T(8,128)(2,1)S(1)}, u32[]{:S(2)}) copy-start(bf16[256,1536]{1,0:T(8,128)(2,1)S(1)} %collective-permute-done.12.refs_6_.refs_3_) | copy-start | bytes 2359300
  25.4 22.6 %collective-permute-start.8 = (bf16[64,1536]{1,0:T(8,128)(2,1)S(1)}, bf16[64,1536]{1,0:T(8,128)(2,1)S(1)}, u32[]{:S(2)}, u32[]{:S(2)}) collective-permute-start(bf16[64,1536]{1,0:T(8,128)(2,1)S(1)} %collective-permute-done.6.v2), channel_id=1, source_target_pairs={{0,4},{1,5},{4,8},{5,9},{6,2},{7,3},{8,12},{9,13},{10,6},{11,7},{1... | collective-permute-start | bytes 589832 | tf_op jit(solution)/shard_map/ppermute | solution.py:193
  28.1 1.3 %copy-start.1 = (bf16[256,1536]{1,0:T(8,128)(2,1)}, bf16[256,1536]{1,0:T(8,128)(2,1)S(1)}, u32[]{:S(2)}) copy-start(bf16[256,1536]{1,0:T(8,128)(2,1)S(1)} %collective-permute-done.13.refs_8_.refs_5_) | copy-start | bytes 2359300
  28.1 23.6 %collective-permute-start.2 = (bf16[64,1536]{1,0:T(8,128)(2,1)S(1)}, bf16[64,1536]{1,0:T(8,128)(2,1)S(1)}, u32[]{:S(2)}, u32[]{:S(2)}) collective-permute-start(bf16[64,1536]{1,0:T(8,128)(2,1)S(1)} %collective-permute-done.1.k2), channel_id=1, source_target_pairs={{0,1},{3,2},{4,5},{7,6},{8,9},{11,10},{12,13},{15,14},{16,17},{19,... | collective-permute-start | bytes 589832 | tf_op jit(solution)/shard_map/ppermute | solution.py:193
  36.4 6.4 %copy-start.16 = (bf16[64,1664]{1,0:T(8,128)(2,1)S(1)}, bf16[64,1664]{1,0:T(8,128)(2,1)}, u32[]{:S(2)}) copy-start(bf16[64,1664]{1,0:T(8,128)(2,1)} %get-tuple-element.7) | copy-start | bytes 638980
  42.8 11.6 %copy-start.6 = (bf16[64,1536]{1,0:T(8,128)(2,1)}, bf16[64,1536]{1,0:T(8,128)(2,1)S(1)}, u32[]{:S(2)}) copy-start(bf16[64,1536]{1,0:T(8,128)(2,1)S(1)} %collective-permute-done.k1) | copy-start | bytes 589828
  42.8 17.7 %collective-permute-start.14 = (bf16[64,1664]{1,0:T(8,128)(2,1)S(1)}, bf16[64,1664]{1,0:T(8,128)(2,1)S(1)}, u32[]{:S(2)}, u32[]{:S(2)}) collective-permute-start(bf16[64,1664]{1,0:T(8,128)(2,1)S(1)} %copy-done.16), channel_id=1, source_target_pairs={{0,2},{1,3},{2,0},{3,1},{4,6},{5,7},{6,4},{7,5},{8,10},{9,11},{10,... | collective-permute-start | bytes 638984 | tf_op jit(solution)/shard_map/ppermute | solution.py:193
  43.4 11.0 %copy-start.7 = (bf16[64,1536]{1,0:T(8,128)(2,1)}, bf16[64,1536]{1,0:T(8,128)(2,1)S(1)}, u32[]{:S(2)}) copy-start(bf16[64,1536]{1,0:T(8,128)(2,1)S(1)} %collective-permute-done.5.v1) | copy-start | bytes 589828
  43.4 17.0 %collective-permute-start.17 = (bf16[64,1664]{1,0:T(8,128)(2,1)}, bf16[64,1664]{1,0:T(8,128)(2,1)S(1)}, u32[]{:S(2)}, u32[]{:S(2)}) collective-permute-start(bf16[64,1664]{1,0:T(8,128)(2,1)} %shard_map.115), channel_id=1, source_target_pairs={{2,4},{3,5},{4,2},{5,3},{6,8},{7,9},{8,6},{9,7},{10,12},{11,13},{1... | collective-permute-start | bytes 638984 | tf_op jit(solution)/shard_map/ppermute | solution.py:193
  46.7 7.7 %copy-start.8 = (bf16[64,1536]{1,0:T(8,128)(2,1)}, bf16[64,1536]{1,0:T(8,128)(2,1)S(1)}, u32[]{:S(2)}) copy-start(bf16[64,1536]{1,0:T(8,128)(2,1)S(1)} %collective-permute-done.3.k4) | copy-start | bytes 589828
  46.7 7.6 %collective-permute-start.7 = (bf16[64,1536]{1,0:T(8,128)(2,1)S(1)}, bf16[64,1536]{1,0:T(8,128)(2,1)S(1)}, u32[]{:S(2)}, u32[]{:S(2)}) collective-permute-start(bf16[64,1536]{1,0:T(8,128)(2,1)S(1)} %collective-permute-done.6.v2), channel_id=1, source_target_pairs={{0,1},{3,2},{4,5},{7,6},{8,9},{11,10},{12,13},{15,14},{16,17},{19,... | collective-permute-start | bytes 589832 | tf_op jit(solution)/shard_map/ppermute | solution.py:193
  48.0 6.3 %copy-start.9 = (bf16[64,1536]{1,0:T(8,128)(2,1)}, bf16[64,1536]{1,0:T(8,128)(2,1)S(1)}, u32[]{:S(2)}) copy-start(bf16[64,1536]{1,0:T(8,128)(2,1)S(1)} %collective-permute-done.8.v4) | copy-start | bytes 589828
  48.1 6.3 %collective-permute-start.4 = (bf16[64,1536]{1,0:T(8,128)(2,1)S(1)}, bf16[64,1536]{1,0:T(8,128)(2,1)S(1)}, u32[]{:S(2)}, u32[]{:S(2)}) collective-permute-start(bf16[64,1536]{1,0:T(8,128)(2,1)S(1)} %collective-permute-done.3.k4), channel_id=1, source_target_pairs={{1,0},{2,3},{5,4},{6,7},{9,8},{10,11},{13,12},{14,15},{17,16},{18,... | collective-permute-start | bytes 589832 | tf_op jit(solution)/shard_map/ppermute | solution.py:193
  51.7 2.7 %copy-start.10 = (bf16[64,1536]{1,0:T(8,128)(2,1)}, bf16[64,1536]{1,0:T(8,128)(2,1)S(1)}, u32[]{:S(2)}) copy-start(bf16[64,1536]{1,0:T(8,128)(2,1)S(1)} %collective-permute-done.2.k3) | copy-start | bytes 589828
  51.7 2.6 %collective-permute-start.9 = (bf16[64,1536]{1,0:T(8,128)(2,1)S(1)}, bf16[64,1536]{1,0:T(8,128)(2,1)S(1)}, u32[]{:S(2)}, u32[]{:S(2)}) collective-permute-start(bf16[64,1536]{1,0:T(8,128)(2,1)S(1)} %collective-permute-done.8.v4), channel_id=1, source_target_pairs={{1,0},{2,3},{5,4},{6,7},{9,8},{10,11},{13,12},{14,15},{17,16},{18,... | collective-permute-start | bytes 589832 | tf_op jit(solution)/shard_map/ppermute | solution.py:193
  54.3 0.7 %copy-start.11 = (bf16[64,1536]{1,0:T(8,128)(2,1)}, bf16[64,1536]{1,0:T(8,128)(2,1)S(1)}, u32[]{:S(2)}) copy-start(bf16[64,1536]{1,0:T(8,128)(2,1)S(1)} %collective-permute-done.7.v3) | copy-start | bytes 589828
  54.3 0.7 %copy-start.12 = (bf16[64,1536]{1,0:T(8,128)(2,1)}, bf16[64,1536]{1,0:T(8,128)(2,1)S(1)}, u32[]{:S(2)}) copy-start(bf16[64,1536]{1,0:T(8,128)(2,1)S(1)} %collective-permute-done.4.k5) | copy-start | bytes 589828
  55.1 0.7 %copy-start.13 = (bf16[64,1536]{1,0:T(8,128)(2,1)}, bf16[64,1536]{1,0:T(8,128)(2,1)S(1)}, u32[]{:S(2)}) copy-start(bf16[64,1536]{1,0:T(8,128)(2,1)S(1)} %collective-permute-done.9.v5) | copy-start | bytes 589828
  60.5 0.7 %copy-start.2 = (bf16[64,1664]{1,0:T(8,128)(2,1)}, bf16[64,1664]{1,0:T(8,128)(2,1)S(1)}, u32[]{:S(2)}) copy-start(bf16[64,1664]{1,0:T(8,128)(2,1)S(1)} %collective-permute-done.14.rx) | copy-start | bytes 638980
  60.5 0.7 %copy-start.3 = (bf16[64,1664]{1,0:T(8,128)(2,1)}, bf16[64,1664]{1,0:T(8,128)(2,1)S(1)}, u32[]{:S(2)}) copy-start(bf16[64,1664]{1,0:T(8,128)(2,1)S(1)} %collective-permute-done.17.rz) | copy-start | bytes 638980
